TPU v7x, 512 devices: a whole 4x8x8 slice. The times are simulated.
512 devices in a mesh: seq: 32 (over x, y), chan: 16 (over z, core).
Axes of the slice: x: 4, y: 8, z: 8, core: 2. Of those that a mesh axis runs over, the one named last changes fastest.
Arguments:
- tokens: bfloat16 [1536, 16384], P('chan', 'seq'), may hold values from -6 to 6
- gate_weight: bfloat16 [1536, 1536], P('chan'), may hold values from -0.15625 to 0.15625
- value_weight: bfloat16 [1536, 1536], P('chan'), may hold values from -0.15625 to 0.15625
- first_factor: bfloat16 [64, 256, 256], P('seq'), may hold values from -0.375 to 0.375
- second_factor: bfloat16 [256, 64, 64], P('seq'), may hold values from -0.75 to 0.75
- down_latent: bfloat16 [1536, 128], P('chan'), may hold values from -0.15625 to 0.15625
- up_latent: bfloat16 [1536, 128], P('chan'), may hold values from -0.5 to 0.5
- doc_lengths: int32 [64], replicated, may hold values from 1 to 8704, 16384 in all
- cotangent: bfloat16 [1536, 16384], P('chan', 'seq'), may hold values from -6 to 6
Outputs:
- hidden: bfloat16 [1536, 16384], P('chan', 'seq')
- d_gate_weight: float32 [1536, 1536], P('chan')
- d_value_weight: float32 [1536, 1536], P('chan')
- d_first: float32 [64, 256, 256], P('seq', 'chan')
- d_second: float32 [256, 64, 64], P('seq', 'chan')
- d_down: float32 [1536, 128], P('chan')
- d_up: float32 [1536, 128], P('chan')
Inputs may be any that keep to these rules, and one draw needn't show every extreme that they name: `doc_lengths`: the documents' lengths sum to 16384; the longest is exactly 8704 tokens.
All inputs are finite; a program needn't handle non-finite values.
Results may differ from a plain program's by a relative error of at most 0.0058.
Values may be sent and summed in bfloat16 or wider, within the bound.
No kernel may reach another device: no remote copies, remote signals or barrier semaphores. Data moves between devices by JAX's collectives and lax.ppermute only.
A program may use at most 64 MiB of HBM per device.

v0:
```python
import jax
import jax.numpy as jnp
from jax import lax
from jax.sharding import PartitionSpec as P

HIGHEST = lax.Precision.HIGHEST


def seq_exchange(x):
    return lax.all_to_all(x, "seq", 0, 0, tiled=True)


def chan_exchange(x):
    return lax.all_to_all(x, "chan", 0, 0, tiled=True)


def split_hi_lo(x):
    hi = lax.reduce_precision(x, exponent_bits=8, mantissa_bits=7)
    lo = x - hi
    return jnp.concatenate([hi.astype(jnp.bfloat16), lo.astype(jnp.bfloat16)], axis=-1)


def join_hi_lo(x):
    n = x.shape[-1] // 2
    return x[..., :n].astype(jnp.float32) + x[..., n:].astype(jnp.float32)


def body(
    tokens,
    gate_weight,
    value_weight,
    first_factor,
    second_factor,
    down_latent,
    up_latent,
    doc_lengths,
    cotangent,
):
    n_seq = lax.axis_size("seq")
    n_chan = lax.axis_size("chan")
    chan_rows, tok_cols = tokens.shape
    blocks_here, block_width, _ = first_factor.shape
    k_here, n_blk2, _ = second_factor.shape
    lat = down_latent.shape[1]
    n_doc = doc_lengths.shape[0]
    docs_here = n_doc // n_seq
    me = lax.axis_index("seq")
    packed = jnp.concatenate([tokens, down_latent], axis=1)
    gathered_all = lax.all_gather(packed, "chan", axis=0, tiled=True)
    gathered = gathered_all[:, :tok_cols]
    down_full = gathered_all[:, tok_cols:]
    doc_ends = jnp.cumsum(doc_lengths)
    doc_begins = doc_ends - doc_lengths
    position = me * tok_cols + jnp.arange(tok_cols, dtype=jnp.int32)
    member = (
        (position[None, :] >= doc_begins[:, None]) & (position[None, :] < doc_ends[:, None])
    ).astype(jnp.float32)
    len_scale = lax.rsqrt(doc_lengths.astype(jnp.float32))
    gate_pre = jnp.dot(gate_weight, gathered, preferred_element_type=jnp.float32)
    value_bf = jnp.dot(value_weight, gathered, preferred_element_type=jnp.float32).astype(
        jnp.bfloat16
    )
    latent = jnp.einsum("ct,cl->lt", gathered, down_full, preferred_element_type=jnp.float32)
    doc_lat_part = jnp.einsum("dt,lt->dl", member, latent, precision=HIGHEST)
    xdoc_part = jnp.einsum(
        "ct,dt->cd", tokens, member.astype(jnp.bfloat16), preferred_element_type=jnp.float32
    )
    blocked = value_bf.reshape(chan_rows, blocks_here, block_width)
    inner_mix = jnp.einsum(
        "ikj,cij->ikc", first_factor, blocked, preferred_element_type=jnp.float32
    ).astype(jnp.bfloat16)
    sig = jax.nn.sigmoid(gate_pre)
    act = gate_pre * sig
    upstream = cotangent.astype(jnp.float32)
    d_mixed = upstream * act
    d_mixed_bf = d_mixed.astype(jnp.bfloat16)
    per_doc_part = jnp.einsum("ct,dt->cd", d_mixed, member, precision=HIGHEST)
    inner_send = inner_mix.reshape(blocks_here, n_seq, k_here, chan_rows).transpose(1, 0, 2, 3)
    d_send = d_mixed_bf.reshape(chan_rows, blocks_here, n_seq, k_here).transpose(2, 1, 3, 0)
    mix_send = jnp.concatenate([inner_send, d_send], axis=3).reshape(n_seq, -1)
    n_mix = mix_send.shape[1]
    small_send = jnp.concatenate(
        [
            doc_lat_part.reshape(n_seq, docs_here * lat),
            per_doc_part.reshape(chan_rows, n_seq, docs_here)
            .transpose(1, 0, 2)
            .reshape(n_seq, chan_rows * docs_here),
            xdoc_part.reshape(chan_rows, n_seq, docs_here)
            .transpose(1, 0, 2)
            .reshape(n_seq, chan_rows * docs_here),
        ],
        axis=1,
    )
    recv2 = seq_exchange(jnp.concatenate([mix_send, split_hi_lo(small_send)], axis=1))
    mix2 = recv2[:, :n_mix].reshape(n_seq, blocks_here, k_here, 2 * chan_rows)
    columns = mix2[..., :chan_rows].reshape(n_seq * blocks_here, k_here, chan_rows)
    d_outer = mix2[..., chan_rows:].reshape(n_seq * blocks_here, k_here, chan_rows)
    small_red = jnp.sum(join_hi_lo(recv2[:, n_mix:]), axis=0)
    n_a = docs_here * lat
    n_b = chan_rows * docs_here
    scale_here = lax.dynamic_slice(len_scale, (me * docs_here,), (docs_here,))
    pooled_here = small_red[:n_a].reshape(docs_here, lat) * scale_here[:, None]
    per_doc_here = small_red[n_a : n_a + n_b].reshape(chan_rows, docs_here)
    xdoc_here = small_red[n_a + n_b :].reshape(chan_rows, docs_here)
    up_float = up_latent.astype(jnp.float32)
    g_part = jnp.einsum("cd,cl->dl", per_doc_here, up_float, precision=HIGHEST)
    outer_mix = jnp.einsum(
        "kmi,ikc->mkc", second_factor, columns, preferred_element_type=jnp.float32
    ).astype(jnp.bfloat16)
    d_inner = jnp.einsum(
        "kmi,mkc->ikc", second_factor, d_outer, preferred_element_type=jnp.float32
    ).astype(jnp.bfloat16)
    d_second_part = jnp.einsum("mkc,ikc->kmi", d_outer, columns, preferred_element_type=jnp.float32)
    outer_send = outer_mix.reshape(n_seq, blocks_here, k_here, chan_rows)
    dinner_send = d_inner.reshape(n_seq, blocks_here, k_here, chan_rows)
    piece = jnp.concatenate(
        [
            pooled_here.reshape(n_a),
            per_doc_here.reshape(n_b),
            xdoc_here.reshape(n_b),
            g_part.reshape(n_a),
        ]
    )
    piece_b = jnp.broadcast_to(split_hi_lo(piece)[None, :], (n_seq, 2 * piece.shape[0]))
    send3 = jnp.concatenate(
        [jnp.concatenate([outer_send, dinner_send], axis=3).reshape(n_seq, -1), piece_b], axis=1
    )
    recv3_all = seq_exchange(send3)
    recv3 = recv3_all[:, :n_mix].reshape(n_seq, blocks_here, k_here, 2 * chan_rows)
    gath3 = join_hi_lo(recv3_all[:, n_mix:])
    outer_tok = (
        recv3[..., :chan_rows]
        .transpose(3, 1, 0, 2)
        .reshape(chan_rows, tok_cols)
        .astype(jnp.float32)
    )
    d_rows = (
        recv3[..., chan_rows:].transpose(1, 0, 2, 3).reshape(blocks_here, n_seq * k_here, chan_rows)
    )
    pooled = gath3[:, :n_a].reshape(n_doc, lat)
    per_doc = (
        gath3[:, n_a : n_a + n_b]
        .reshape(n_seq, chan_rows, docs_here)
        .transpose(1, 0, 2)
        .reshape(chan_rows, n_doc)
    )
    xdoc = (
        gath3[:, n_a + n_b : n_a + 2 * n_b]
        .reshape(n_seq, chan_rows, docs_here)
        .transpose(1, 0, 2)
        .reshape(chan_rows, n_doc)
    )
    g_gath = gath3[:, n_a + 2 * n_b :].reshape(1, n_doc * lat)
    spread = jnp.einsum("dl,cl->cd", pooled, up_float, precision=HIGHEST)
    summary = jnp.dot(spread, member, precision=HIGHEST)
    mixed = outer_tok + summary
    hidden = (act * mixed).astype(jnp.bfloat16)
    d_gate_bf = (upstream * mixed * sig * (1.0 + gate_pre * (1.0 - sig))).astype(jnp.bfloat16)
    d_value_bf = (
        jnp.einsum("ikj,ikc->cij", first_factor, d_rows, preferred_element_type=jnp.float32)
        .astype(jnp.bfloat16)
        .reshape(chan_rows, tok_cols)
    )
    d_first_part = jnp.einsum("ikc,cij->ikj", d_rows, blocked, preferred_element_type=jnp.float32)
    d_up = jnp.einsum("cd,dl->cl", per_doc, pooled, precision=HIGHEST)
    both_grads = jnp.concatenate([d_gate_bf, d_value_bf], axis=0)
    d_proj_part = jnp.einsum("ot,it->oi", both_grads, gathered, preferred_element_type=jnp.float32)
    rows_here = 2 * chan_rows // n_seq
    width = d_proj_part.shape[1]
    proj_send = d_proj_part.reshape(n_seq, rows_here, width).astype(jnp.bfloat16)
    proj_red = jnp.sum(seq_exchange(proj_send).astype(jnp.float32), axis=0)
    k_part = block_width // n_chan
    m_part = n_blk2 // n_chan
    first_send = (
        d_first_part.reshape(blocks_here, n_chan, k_part, block_width)
        .transpose(1, 0, 2, 3)
        .reshape(n_chan, -1)
    )
    second_send = (
        d_second_part.reshape(k_here, n_chan, m_part, n_blk2)
        .transpose(1, 0, 2, 3)
        .reshape(n_chan, -1)
    )
    g_send = jnp.broadcast_to(g_gath, (n_chan, n_doc * lat))
    fac_send = jnp.concatenate([first_send, second_send, g_send], axis=1)
    fac_red = lax.psum_scatter(
        fac_send.reshape(-1, 128), "chan", scatter_dimension=0, tiled=True
    ).reshape(-1)
    n_f = blocks_here * k_part * block_width
    d_first = fac_red[:n_f].reshape(blocks_here, k_part, block_width)
    n_s = k_here * m_part * n_blk2
    d_second = fac_red[n_f : n_f + n_s].reshape(k_here, m_part, n_blk2)
    g_full = fac_red[n_f + n_s :].reshape(n_doc, lat)
    gath5 = seq_exchange(jnp.broadcast_to(proj_red[None], (n_seq, rows_here, width)))
    d_proj = gath5.reshape(2 * chan_rows, width)
    d_pooled = g_full * len_scale[:, None]
    d_down = jnp.einsum(
        "cd,dl->cl", xdoc, d_pooled.astype(jnp.bfloat16).astype(jnp.float32), precision=HIGHEST
    )
    return (hidden, d_proj[:chan_rows], d_proj[chan_rows:], d_first, d_second, d_down, d_up)


def solution(mesh):
    in_specs = (
        P("chan", "seq"),
        P("chan", None),
        P("chan", None),
        P("seq", None, None),
        P("seq", None, None),
        P("chan", None),
        P("chan", None),
        P(),
        P("chan", "seq"),
    )
    out_specs = (
        P("chan", "seq"),
        P("chan", None),
        P("chan", None),
        P("seq", "chan", None),
        P("seq", "chan", None),
        P("chan", None),
        P("chan", None),
    )
    return jax.shard_map(body, mesh=mesh, in_specs=in_specs, out_specs=out_specs, check_vma=False)
```

profile of v0, /device:TPU:6, one launch (start us, length us, event | category | flops | bytes accessed | tf_op | source)
XLA Modules:
  0.0 200.5 jit_solution(10429211262752419553)
XLA Ops:
  7.2 1.6 pad_maximum_fusion.2
  8.9 0.7 copy.85
  9.9 0.7 sub.12
  10.5 1.1 fusion.27
  11.8 46.3 %all-gather.2.cloned.1.call-done = bf16[1536,640]{1,0:T(8,128)(2,1)} async-done(((bf16[96,640]{1,0:T(8,128)(2,1)}), bf16[1536,640]{1,0:T(8,128)(2,1)}) %all-gather.2.cloned.1.call-update) | async-done | bytes 1966096 | tf_op jit(solution)/shard_map/all_gather | solution.py:49
  58.1 1.9 convolution_convert_fusion.3
  60.0 0.2 fusion
  60.4 2.0 fusion.3
  62.3 0.3 fusion.35
  62.7 1.8 fusion.16
  64.8 0.2 reshape.192
  65.1 0.3 fusion.15
  65.7 0.5 broadcast.29
  66.2 0.8 reduce.1
  67.0 0.8 reshape.228
  67.8 9.9 %all-to-all-start = ((bf16[32,2,2176]{2,1,0:T(2,128)(2,1)}), bf16[32,2,2176]{2,1,0:T(2,128)(2,1)S(1)}, u32[]{:S(2)}, u32[]{:S(2)}) async-start(bf16[32,2,2176]{2,1,0:T(2,128)(2,1)} %reshape.228), calls=%async_computation | async-start | bytes 557056 | tf_op jit(solution)/shard_map/all_to_all | solution.py:10
  77.8 11.0 %all-to-all-done = bf16[32,2,2176]{2,1,0:T(2,128)(2,1)S(1)} async-done(((bf16[32,2,2176]{2,1,0:T(2,128)(2,1)}), bf16[32,2,2176]{2,1,0:T(2,128)(2,1)S(1)}, u32[]{:S(2)}, u32[]{:S(2)}) %all-to-all-start) | async-done | bytes 278560 | tf_op jit(solution)/shard_map/all_to_all | solution.py:10
  88.8 0.2 reshape.229
  89.4 0.3 reshape.200
  90.4 0.2 convolution_convert_fusion.2
  90.9 0.3 reshape.205
  91.5 0.8 reduce.2
  92.3 0.8 reshape.230
  93.1 6.5 %all-to-all-start.1 = ((bf16[32,2,2432]{2,1,0:T(2,128)(2,1)}), bf16[32,2,2432]{2,1,0:T(2,128)(2,1)S(1)}, u32[]{:S(2)}, u32[]{:S(2)}) async-start(bf16[32,2,2432]{2,1,0:T(2,128)(2,1)} %reshape.230), calls=%async_computation.1 | async-start | bytes 622592 | tf_op jit(solution)/shard_map/all_to_all | solution.py:10
  99.9 0.2 reshape.216
  100.1 10.5 %all-to-all-done.1 = bf16[32,2,2432]{2,1,0:T(2,128)(2,1)S(1)} async-done(((bf16[32,2,2432]{2,1,0:T(2,128)(2,1)}), bf16[32,2,2432]{2,1,0:T(2,128)(2,1)S(1)}, u32[]{:S(2)}, u32[]{:S(2)}) %all-to-all-start.1) | async-done | bytes 311328 | tf_op jit(solution)/shard_map/all_to_all | solution.py:10
  110.6 0.3 reshape.231
  111.0 0.3 reshape.209
  111.4 0.2 fusion.1
  111.6 0.2 fusion.17
  112.3 1.0 fusion.10
  113.3 2.1 %convolution_convert_fusion = bf16[192,1536]{1,0:T(8,128)(2,1)S(1)} fusion(bf16[1536,640]{1,0:T(8,128)(2,1)} %all-gather.2.cloned.1.call-done, bf16[96,512]{1,0:T(8,128)(2,1)S(1)} %bitcast.139, bf16[96,512]{1,0:T(8,128)(2,1)S(1)} %get-tuple-element.9), kind=kOutput, calls=%fused_computation | convolution fusion | flops 302678016 | bytes 2359296 | tf_op jit(solution)/shard_map/ot,it->oi/dot_general | solution.py:167
  115.4 1.1 convert_element_type.128
  116.4 6.6 %all-to-all-start.2 = ((bf16[32,6,1536]{2,1,0:T(8,128)(2,1)}), bf16[32,6,1536]{2,1,0:T(8,128)(2,1)S(1)}, u32[]{:S(2)}, u32[]{:S(2)}) async-start(bf16[32,6,1536]{2,1,0:T(8,128)(2,1)} %convert_element_type.128), calls=%async_computation.2 | async-start | bytes 1572864 | tf_op jit(solution)/shard_map/all_to_all | solution.py:10
  123.1 0.3 copy.117
  123.5 1.2 reshape.217
  124.8 17.8 %all-to-all-done.2 = bf16[32,6,1536]{2,1,0:T(8,128)(2,1)S(1)} async-done(((bf16[32,6,1536]{2,1,0:T(8,128)(2,1)}), bf16[32,6,1536]{2,1,0:T(8,128)(2,1)S(1)}, u32[]{:S(2)}, u32[]{:S(2)}) %all-to-all-start.2) | async-done | bytes 589856 | tf_op jit(solution)/shard_map/all_to_all | solution.py:10
  142.8 1.3 broadcast_in_dim.9
  144.1 7.3 %all-to-all-start.3 = ((f32[32,6,1536]{2,1,0:T(8,128)}), f32[32,6,1536]{2,1,0:T(8,128)S(1)}, u32[]{:S(2)}, u32[]{:S(2)}) async-start(f32[32,6,1536]{2,1,0:T(8,128)} %broadcast_in_dim.9), calls=%async_computation.3 | async-start | bytes 3145728 | tf_op jit(solution)/shard_map/all_to_all | solution.py:10
  151.9 0.9 fusion.42
  152.8 34.6 %reduce-scatter.2.cloned.1.call-done = f32[144,128]{1,0:T(8,128)} async-done(((f32[2304,128]{1,0:T(8,128)}), f32[144,128]{1,0:T(8,128)}) %reduce-scatter.2.cloned.1.call-update) | async-done | bytes 73744 | tf_op jit(solution)/shard_map/reduce_scatter | solution.py:186
  187.3 0.7 slice.150
  188.0 0.7 reshape.219
  188.7 0.8 slice.149
  189.5 0.6 reshape.218
  190.1 1.6 fusion.29
  191.8 0.9 slice.126
  192.7 0.9 slice.124
  (74 shorter events, 4.4 us)
Async XLA Ops:
  7.2 55.5 %copy-start = (bf16[96,1536]{1,0:T(8,128)(2,1)S(1)}, bf16[96,1536]{1,0:T(8,128)(2,1)}, u32[]{:S(2)}) copy-start(bf16[96,1536]{1,0:T(8,128)(2,1)} %param.10) | copy-start | bytes 884740
  7.2 52.8 %copy-start.1 = (bf16[2,256,256]{2,1,0:T(8,128)(2,1)S(1)}, bf16[2,256,256]{2,1,0:T(8,128)(2,1)}, u32[]{:S(2)}) copy-start(bf16[2,256,256]{2,1,0:T(8,128)(2,1)} %param.12) | copy-start | bytes 786436
  7.2 50.9 %all-gather.2.cloned.1.call-start = ((), (), s32[]{:S(2)}) async-start(), calls=%async_computation.5 | async-start | bytes 2088960 | tf_op jit(solution)/shard_map/all_gather | solution.py:49
  60.0 2.6 %copy-start.5 = (bf16[96,512]{1,0:T(8,128)(2,1)S(1)}, bf16[96,512]{1,0:T(8,128)(2,1)}, u32[]{:S(2)}) copy-start(bf16[96,512]{1,0:T(8,128)(2,1)} %param.17) | copy-start | bytes 294916
  65.4 12.3 %copy-start.4 = (s32[64]{0:T(128)S(1)}, s32[64]{0:T(128)}, u32[]{:S(2)}) copy-start(s32[64]{0:T(128)} %param.16) | copy-start | bytes 772
  67.8 21.0 %all-to-all-start = ((bf16[32,2,2176]{2,1,0:T(2,128)(2,1)}), bf16[32,2,2176]{2,1,0:T(2,128)(2,1)S(1)}, u32[]{:S(2)}, u32[]{:S(2)}) async-start(bf16[32,2,2176]{2,1,0:T(2,128)(2,1)} %reshape.228), calls=%async_computation | async-start | bytes 557056 | tf_op jit(solution)/shard_map/all_to_all | solution.py:10
  77.8 12.1 %copy-start.2 = (bf16[8,64,64]{2,1,0:T(8,128)(2,1)S(1)}, bf16[8,64,64]{2,1,0:T(8,128)(2,1)}, u32[]{:S(2)}) copy-start(bf16[8,64,64]{2,1,0:T(8,128)(2,1)} %param.13) | copy-start | bytes 196612
  89.7 1.5 copy-start.3
  93.1 17.5 %all-to-all-start.1 = ((bf16[32,2,2432]{2,1,0:T(2,128)(2,1)}), bf16[32,2,2432]{2,1,0:T(2,128)(2,1)S(1)}, u32[]{:S(2)}, u32[]{:S(2)}) async-start(bf16[32,2,2432]{2,1,0:T(2,128)(2,1)} %reshape.230), calls=%async_computation.1 | async-start | bytes 622592 | tf_op jit(solution)/shard_map/all_to_all | solution.py:10
  116.4 26.2 %all-to-all-start.2 = ((bf16[32,6,1536]{2,1,0:T(8,128)(2,1)}), bf16[32,6,1536]{2,1,0:T(8,128)(2,1)S(1)}, u32[]{:S(2)}, u32[]{:S(2)}) async-start(bf16[32,6,1536]{2,1,0:T(8,128)(2,1)} %convert_element_type.128), calls=%async_computation.2 | async-start | bytes 1572864 | tf_op jit(solution)/shard_map/all_to_all | solution.py:10
  123.0 64.3 %reduce-scatter.2.cloned.1.call-start = ((), (), s32[]{:S(2)}) async-start(), calls=%async_computation.6 | async-start | bytes 1253376 | tf_op jit(solution)/shard_map/reduce_scatter | solution.py:186
  144.1 47.6 %all-to-all-start.3 = ((f32[32,6,1536]{2,1,0:T(8,128)}), f32[32,6,1536]{2,1,0:T(8,128)S(1)}, u32[]{:S(2)}, u32[]{:S(2)}) async-start(f32[32,6,1536]{2,1,0:T(8,128)} %broadcast_in_dim.9), calls=%async_computation.3 | async-start | bytes 3145728 | tf_op jit(solution)/shard_map/all_to_all | solution.py:10
Sparse Core Ops, SparseCore 0:
  10.7 47.3 all-gather.1
  126.6 60.6 reduce-scatter.1
where the time goes:
time: 201 us; the launch traced here: 200 us
  waiting for transfers between devices  120 us (60%)
  starting transfers between devices  30.3 us (15%)
  local copies, waits for them, and re-layouts  15.6 us (8%)
  matrix products  14.6 us (7%)
  between operations  14.6 us (7%)
  other arithmetic  5.08 us (3%)
    all_gather x1, waiting for transfers between devices, body(): gathered_all = lax.all_gather(packed, 'chan', axis=0, tiled=True)  46.3 us
    all_to_all x4, waiting for transfers between devices, seq_exchange(): return lax.all_to_all(x, 'seq', 0, 0, tiled=True)  39.4 us
    reduce_scatter x1, waiting for transfers between devices, body(): lax.psum_scatter(fac_send.reshape(-1, 128), 'chan', scatter_dimension=0,...  34.6 us
    all_to_all x4, starting transfers between devices, seq_exchange(): return lax.all_to_all(x, 'seq', 0, 0, tiled=True)  30.2 us
  transfers between devices with their start and end apart: 6, of which 5 were waited for; matrix products, arithmetic and copies ran while one was open for 6% of the time, Pallas kernels for 0%

commit v1 on v0

--- a/solution.py
+++ b/solution.py
@@ -4,6 +4,19 @@
 from jax.sharding import PartitionSpec as P
 
 HIGHEST = lax.Precision.HIGHEST
+
+
+def ring_gather(x, axis, dim):
+    ways = lax.axis_size(axis)
+    up = [(d, (d + 1) % ways) for d in range(ways)]
+    down = [(d, (d - 1) % ways) for d in range(ways)]
+    earlier, later = ([x], [x])
+    for _ in range(ways // 2):
+        earlier.append(lax.ppermute(earlier[-1], axis, up))
+    for _ in range((ways - 1) // 2):
+        later.append(lax.ppermute(later[-1], axis, down))
+    line = jnp.concatenate([*earlier[::-1], *later[1:]], axis=dim)
+    return jnp.roll(line, (lax.axis_index(axis) - ways // 2) * x.shape[dim], axis=dim)
 
 
 def seq_exchange(x):
@@ -46,7 +59,7 @@
     docs_here = n_doc // n_seq
     me = lax.axis_index("seq")
     packed = jnp.concatenate([tokens, down_latent], axis=1)
-    gathered_all = lax.all_gather(packed, "chan", axis=0, tiled=True)
+    gathered_all = ring_gather(packed, "chan", 0)
     gathered = gathered_all[:, :tok_cols]
     down_full = gathered_all[:, tok_cols:]
     doc_ends = jnp.cumsum(doc_lengths)

time: 201 us -> 203 us (level)
  waiting for transfers between devices: 120 us -> 97.6 us
  starting transfers between devices: 30.3 us -> 51.2 us
  local copies, waits for them, and re-layouts: 15.6 us -> 21.5 us
    all_gather x1 -> x0, waiting for transfers between devices: 46.3 us -> none  [body(): gathered_all = lax.all_gather(packed, 'chan', axis=0, tiled=True)]
    ppermute x0 -> x15, waiting for transfers between devices: none -> 25.9 us  [the longest x8 25.7 us: ring_gather(): earlier.append(lax.ppermute(earlier[-1], axis, up))]
    ppermute x0 -> x15, starting transfers between devices: none -> 20.8 us  [the longest x7 20.8 us: ring_gather(): later.append(lax.ppermute(later[-1], axis, down))]
    all_to_all x4, waiting for transfers between devices: 39.4 us -> 31.8 us  [seq_exchange(): return lax.all_to_all(x, 'seq', 0, 0, tiled=True)]
    reduce_scatter x1, waiting for transfers between devices: 34.6 us -> 39.8 us  [body(): lax.psum_scatter(fac_send.reshape(-1, 128), 'chan', scatter_dimension=0,...]
    unnamed x21 -> x63, local copies, waits for them, and re-layouts: 2.51 us -> 7.58 us
  transfers between devices with their start and end apart: 6 -> 20, of which waited for: 5 -> 13; matrix products, arithmetic and copies ran while one was open for 6% -> 7% of each run, Pallas kernels for 0% -> 0%
where the time goes in v1:
time: 203 us; the launch traced here: 202 us
  waiting for transfers between devices  97.6 us (48%)
  starting transfers between devices  51.2 us (25%)
  local copies, waits for them, and re-layouts  21.5 us (11%)
  between operations  14.8 us (7%)
  matrix products  13.8 us (7%)
  other arithmetic  3.43 us (2%)
    reduce_scatter x1, waiting for transfers between devices, body(): lax.psum_scatter(fac_send.reshape(-1, 128), 'chan', scatter_dimension=0,...  39.8 us
    all_to_all x4, waiting for transfers between devices, seq_exchange(): return lax.all_to_all(x, 'seq', 0, 0, tiled=True)  31.8 us
    all_to_all x4, starting transfers between devices, seq_exchange(): return lax.all_to_all(x, 'seq', 0, 0, tiled=True)  30.3 us
    ppermute x8, waiting for transfers between devices, ring_gather(): earlier.append(lax.ppermute(earlier[-1], axis, up))  25.7 us
    ppermute x7, starting transfers between devices, ring_gather(): later.append(lax.ppermute(later[-1], axis, down))  20.8 us
    unnamed x63, local copies, waits for them, and re-layouts  7.58 us
  transfers between devices with their start and end apart: 20, of which 13 were waited for; matrix products, arithmetic and copies ran while one was open for 7% of the time, Pallas kernels for 0%

profile of v1, /device:TPU:6, one launch (start us, length us, event | category | flops | bytes accessed | tf_op | source)
XLA Modules:
  0.0 202.3 jit_solution(3197806652210643433)
XLA Ops:
  7.2 1.0 constant_dynamic-update-slice_fusion.1
  8.2 0.7 constant_dynamic-update-slice_fusion
  8.9 11.0 %collective-permute-done = bf16[96,640]{1,0:T(8,128)(2,1)S(1)} collective-permute-done((bf16[96,640]{1,0:T(8,128)(2,1)S(1)}, bf16[96,640]{1,0:T(8,128)(2,1)S(1)}, u32[]{:S(2)}, u32[]{:S(2)}) %collective-permute-start) | collective-permute-done | bytes 122912 | tf_op jit(solution)/shard_map/ppermute | solution.py:15
  20.0 3.0 %collective-permute-start.8 = (bf16[96,640]{1,0:T(8,128)(2,1)S(1)}, bf16[96,640]{1,0:T(8,128)(2,1)S(1)}, u32[]{:S(2)}, u32[]{:S(2)}) collective-permute-start(bf16[96,640]{1,0:T(8,128)(2,1)S(1)} %constant_dynamic-update-slice_fusion), channel_id=1, source_target_pairs={{0,15},{1,0},{2,1},{3,2},{4,3},{5,4},{6,5},{7,6},{8,7},{9,8},{10,9... | collective-permute-start | bytes 368648 | tf_op jit(solution)/shard_map/ppermute | solution.py:17
  22.9 2.6 %collective-permute-done.1 = bf16[96,640]{1,0:T(8,128)(2,1)S(1)} collective-permute-done((bf16[96,640]{1,0:T(8,128)(2,1)S(1)}, bf16[96,640]{1,0:T(8,128)(2,1)S(1)}, u32[]{:S(2)}, u32[]{:S(2)}) %collective-permute-start.1) | collective-permute-done | bytes 122912 | tf_op jit(solution)/shard_map/ppermute | solution.py:15
  25.5 3.0 %collective-permute-start.9 = (bf16[96,640]{1,0:T(8,128)(2,1)S(1)}, bf16[96,640]{1,0:T(8,128)(2,1)S(1)}, u32[]{:S(2)}, u32[]{:S(2)}) collective-permute-start(bf16[96,640]{1,0:T(8,128)(2,1)S(1)} %collective-permute-done.8), channel_id=1, source_target_pairs={{0,15},{1,0},{2,1},{3,2},{4,3},{5,4},{6,5},{7,6},{8,7},{9,8},{10,9... | collective-permute-start | bytes 368648 | tf_op jit(solution)/shard_map/ppermute | solution.py:17
  28.4 2.6 %collective-permute-done.2 = bf16[96,640]{1,0:T(8,128)(2,1)S(1)} collective-permute-done((bf16[96,640]{1,0:T(8,128)(2,1)S(1)}, bf16[96,640]{1,0:T(8,128)(2,1)S(1)}, u32[]{:S(2)}, u32[]{:S(2)}) %collective-permute-start.2) | collective-permute-done | bytes 122912 | tf_op jit(solution)/shard_map/ppermute | solution.py:15
  31.0 3.0 %collective-permute-start.10 = (bf16[96,640]{1,0:T(8,128)(2,1)S(1)}, bf16[96,640]{1,0:T(8,128)(2,1)S(1)}, u32[]{:S(2)}, u32[]{:S(2)}) collective-permute-start(bf16[96,640]{1,0:T(8,128)(2,1)S(1)} %collective-permute-done.9), channel_id=1, source_target_pairs={{0,15},{1,0},{2,1},{3,2},{4,3},{5,4},{6,5},{7,6},{8,7},{9,8},{10,9... | collective-permute-start | bytes 368648 | tf_op jit(solution)/shard_map/ppermute | solution.py:17
  33.9 2.6 %collective-permute-done.3 = bf16[96,640]{1,0:T(8,128)(2,1)S(1)} collective-permute-done((bf16[96,640]{1,0:T(8,128)(2,1)S(1)}, bf16[96,640]{1,0:T(8,128)(2,1)S(1)}, u32[]{:S(2)}, u32[]{:S(2)}) %collective-permute-start.3) | collective-permute-done | bytes 122912 | tf_op jit(solution)/shard_map/ppermute | solution.py:15
  36.5 3.0 %collective-permute-start.11 = (bf16[96,640]{1,0:T(8,128)(2,1)S(1)}, bf16[96,640]{1,0:T(8,128)(2,1)S(1)}, u32[]{:S(2)}, u32[]{:S(2)}) collective-permute-start(bf16[96,640]{1,0:T(8,128)(2,1)S(1)} %collective-permute-done.10), channel_id=1, source_target_pairs={{0,15},{1,0},{2,1},{3,2},{4,3},{5,4},{6,5},{7,6},{8,7},{9,8},{10,9... | collective-permute-start | bytes 368648 | tf_op jit(solution)/shard_map/ppermute | solution.py:17
  39.5 2.6 %collective-permute-done.4 = bf16[96,640]{1,0:T(8,128)(2,1)S(1)} collective-permute-done((bf16[96,640]{1,0:T(8,128)(2,1)S(1)}, bf16[96,640]{1,0:T(8,128)(2,1)S(1)}, u32[]{:S(2)}, u32[]{:S(2)}) %collective-permute-start.4) | collective-permute-done | bytes 122912 | tf_op jit(solution)/shard_map/ppermute | solution.py:15
  42.0 3.0 %collective-permute-start.12 = (bf16[96,640]{1,0:T(8,128)(2,1)S(1)}, bf16[96,640]{1,0:T(8,128)(2,1)S(1)}, u32[]{:S(2)}, u32[]{:S(2)}) collective-permute-start(bf16[96,640]{1,0:T(8,128)(2,1)S(1)} %collective-permute-done.11), channel_id=1, source_target_pairs={{0,15},{1,0},{2,1},{3,2},{4,3},{5,4},{6,5},{7,6},{8,7},{9,8},{10,9... | collective-permute-start | bytes 368648 | tf_op jit(solution)/shard_map/ppermute | solution.py:17
  45.0 2.6 %collective-permute-done.5 = bf16[96,640]{1,0:T(8,128)(2,1)S(1)} collective-permute-done((bf16[96,640]{1,0:T(8,128)(2,1)S(1)}, bf16[96,640]{1,0:T(8,128)(2,1)S(1)}, u32[]{:S(2)}, u32[]{:S(2)}) %collective-permute-start.5) | collective-permute-done | bytes 122912 | tf_op jit(solution)/shard_map/ppermute | solution.py:15
  47.5 0.7 copy.85
  49.2 3.0 %collective-permute-start.13 = (bf16[96,640]{1,0:T(8,128)(2,1)S(1)}, bf16[96,640]{1,0:T(8,128)(2,1)S(1)}, u32[]{:S(2)}, u32[]{:S(2)}) collective-permute-start(bf16[96,640]{1,0:T(8,128)(2,1)S(1)} %collective-permute-done.12), channel_id=1, source_target_pairs={{0,15},{1,0},{2,1},{3,2},{4,3},{5,4},{6,5},{7,6},{8,7},{9,8},{10,9... | collective-permute-start | bytes 368648 | tf_op jit(solution)/shard_map/ppermute | solution.py:17
  52.1 0.9 collective-permute-done.6
  53.0 1.1 fusion.27
  54.6 3.1 %collective-permute-start.14 = (bf16[96,640]{1,0:T(8,128)(2,1)S(1)}, bf16[96,640]{1,0:T(8,128)(2,1)S(1)}, u32[]{:S(2)}, u32[]{:S(2)}) collective-permute-start(bf16[96,640]{1,0:T(8,128)(2,1)S(1)} %collective-permute-done.13), channel_id=1, source_target_pairs={{0,15},{1,0},{2,1},{3,2},{4,3},{5,4},{6,5},{7,6},{8,7},{9,8},{10,9... | collective-permute-start | bytes 368648 | tf_op jit(solution)/shard_map/ppermute | solution.py:17
  57.6 0.9 collective-permute-done.7
  58.8 0.9 constant_dynamic-update-slice_fusion.25
  59.7 0.7 constant_dynamic-update-slice_fusion.35
  61.1 1.8 copy-done.1
  63.7 2.0 convolution_convert_fusion.3
  66.9 2.4 %fusion.3 = f32[128,512]{1,0:T(8,128)S(1)} fusion(bf16[3072,640]{1,0:T(8,128)(2,1)} %copy-done.1, s32[]{:T(128)S(6)} %select_n.17, s32[]{:T(128)S(6)} %add.52), kind=kOutput, calls=%fused_computation.14 | convolution fusion | flops 201326592 | bytes 2229760 | tf_op jit(solution)/shard_map/ct,cl->lt/dot_general | solution.py:76
  70.3 0.8 reduce.1
  71.1 0.8 reshape.228
  71.8 10.2 %all-to-all-start = ((bf16[32,2,2176]{2,1,0:T(2,128)(2,1)}), bf16[32,2,2176]{2,1,0:T(2,128)(2,1)S(1)}, u32[]{:S(2)}, u32[]{:S(2)}) async-start(bf16[32,2,2176]{2,1,0:T(2,128)(2,1)} %reshape.228), calls=%async_computation | async-start | bytes 557056 | tf_op jit(solution)/shard_map/all_to_all | solution.py:23
  82.2 9.2 %all-to-all-done = bf16[32,2,2176]{2,1,0:T(2,128)(2,1)S(1)} async-done(((bf16[32,2,2176]{2,1,0:T(2,128)(2,1)}), bf16[32,2,2176]{2,1,0:T(2,128)(2,1)S(1)}, u32[]{:S(2)}, u32[]{:S(2)}) %all-to-all-start) | async-done | bytes 278560 | tf_op jit(solution)/shard_map/all_to_all | solution.py:23
  94.0 0.8 reduce.2
  94.8 0.8 reshape.230
  95.6 6.4 %all-to-all-start.1 = ((bf16[32,2,2432]{2,1,0:T(2,128)(2,1)}), bf16[32,2,2432]{2,1,0:T(2,128)(2,1)S(1)}, u32[]{:S(2)}, u32[]{:S(2)}) async-start(bf16[32,2,2432]{2,1,0:T(2,128)(2,1)} %reshape.230), calls=%async_computation.1 | async-start | bytes 622592 | tf_op jit(solution)/shard_map/all_to_all | solution.py:23
  102.5 9.2 %all-to-all-done.1 = bf16[32,2,2432]{2,1,0:T(2,128)(2,1)S(1)} async-done(((bf16[32,2,2432]{2,1,0:T(2,128)(2,1)}), bf16[32,2,2432]{2,1,0:T(2,128)(2,1)S(1)}, u32[]{:S(2)}, u32[]{:S(2)}) %all-to-all-start.1) | async-done | bytes 311328 | tf_op jit(solution)/shard_map/all_to_all | solution.py:23
  113.7 1.0 fusion.10
  114.7 2.1 %convolution_convert_fusion = bf16[192,1536]{1,0:T(8,128)(2,1)S(1)} fusion(bf16[3072,640]{1,0:T(8,128)(2,1)} %copy-done.1, s32[]{:T(128)S(6)} %select_n.17, bf16[96,512]{1,0:T(8,128)(2,1)S(1)} %bitcast.132, bf16[96,512]{1,0:T(8,128)(2,1)S(1)} %get-tuple-element.9), kind=kOutput, calls=%fused_computation | convolution fusion | flops 302678016 | bytes 2359300 | tf_op jit(solution)/shard_map/ot,it->oi/dot_general | solution.py:180
  116.8 1.1 convert_element_type.128
  117.9 6.2 %all-to-all-start.2 = ((bf16[32,6,1536]{2,1,0:T(8,128)(2,1)}), bf16[32,6,1536]{2,1,0:T(8,128)(2,1)S(1)}, u32[]{:S(2)}, u32[]{:S(2)}) async-start(bf16[32,6,1536]{2,1,0:T(8,128)(2,1)} %convert_element_type.128), calls=%async_computation.2 | async-start | bytes 1572864 | tf_op jit(solution)/shard_map/all_to_all | solution.py:23
  124.3 1.2 reshape.217
  125.6 13.4 %all-to-all-done.2 = bf16[32,6,1536]{2,1,0:T(8,128)(2,1)S(1)} async-done(((bf16[32,6,1536]{2,1,0:T(8,128)(2,1)}), bf16[32,6,1536]{2,1,0:T(8,128)(2,1)S(1)}, u32[]{:S(2)}, u32[]{:S(2)}) %all-to-all-start.2) | async-done | bytes 589856 | tf_op jit(solution)/shard_map/all_to_all | solution.py:23
  139.2 1.3 broadcast_in_dim.9
  140.5 7.4 %all-to-all-start.3 = ((f32[32,6,1536]{2,1,0:T(8,128)}), f32[32,6,1536]{2,1,0:T(8,128)S(1)}, u32[]{:S(2)}, u32[]{:S(2)}) async-start(f32[32,6,1536]{2,1,0:T(8,128)} %broadcast_in_dim.9), calls=%async_computation.3 | async-start | bytes 3145728 | tf_op jit(solution)/shard_map/all_to_all | solution.py:23
  148.4 0.9 fusion.46
  149.3 39.8 %reduce-scatter.2.cloned.1.call-done = f32[144,128]{1,0:T(8,128)} async-done(((f32[2304,128]{1,0:T(8,128)}), f32[144,128]{1,0:T(8,128)}) %reduce-scatter.2.cloned.1.call-update) | async-done | bytes 73744 | tf_op jit(solution)/shard_map/reduce_scatter | solution.py:199
  189.1 0.8 slice.147
  190.5 0.7 slice.148
  191.2 0.7 reshape.219
  191.9 1.6 fusion.29
  193.6 0.9 slice.124
  194.5 0.9 slice.126
  (144 shorter events, 11.3 us)
Async XLA Ops:
  7.2 55.7 %copy-start = (bf16[96,1536]{1,0:T(8,128)(2,1)S(1)}, bf16[96,1536]{1,0:T(8,128)(2,1)}, u32[]{:S(2)}) copy-start(bf16[96,1536]{1,0:T(8,128)(2,1)} %param.10) | copy-start | bytes 884740
  7.2 53.6 %copy-start.3 = (bf16[96,512]{1,0:T(8,128)(2,1)S(1)}, bf16[96,512]{1,0:T(8,128)(2,1)}, u32[]{:S(2)}) copy-start(bf16[96,512]{1,0:T(8,128)(2,1)} %param.9) | copy-start | bytes 294916
  7.2 53.6 %copy-start.6 = (bf16[96,128]{1,0:T(8,128)(2,1)S(1)}, bf16[96,128]{1,0:T(8,128)(2,1)}, u32[]{:S(2)}) copy-start(bf16[96,128]{1,0:T(8,128)(2,1)} %param.14) | copy-start | bytes 73732
  8.9 11.0 %collective-permute-start = (bf16[96,640]{1,0:T(8,128)(2,1)S(1)}, bf16[96,640]{1,0:T(8,128)(2,1)S(1)}, u32[]{:S(2)}, u32[]{:S(2)}) collective-permute-start(bf16[96,640]{1,0:T(8,128)(2,1)S(1)} %constant_dynamic-update-slice_fusion), channel_id=1, source_target_pairs={{0,1},{1,2},{2,3},{3,4},{4,5},{5,6},{6,7},{7,8},{8,9},{9,10},{10,1... | collective-permute-start | bytes 368648 | tf_op jit(solution)/shard_map/ppermute | solution.py:15
  19.9 5.5 %collective-permute-start.1 = (bf16[96,640]{1,0:T(8,128)(2,1)S(1)}, bf16[96,640]{1,0:T(8,128)(2,1)S(1)}, u32[]{:S(2)}, u32[]{:S(2)}) collective-permute-start(bf16[96,640]{1,0:T(8,128)(2,1)S(1)} %collective-permute-done), channel_id=1, source_target_pairs={{0,1},{1,2},{2,3},{3,4},{4,5},{5,6},{6,7},{7,8},{8,9},{9,10},{10,1... | collective-permute-start | bytes 368648 | tf_op jit(solution)/shard_map/ppermute | solution.py:15
  20.0 5.5 %collective-permute-start.8 = (bf16[96,640]{1,0:T(8,128)(2,1)S(1)}, bf16[96,640]{1,0:T(8,128)(2,1)S(1)}, u32[]{:S(2)}, u32[]{:S(2)}) collective-permute-start(bf16[96,640]{1,0:T(8,128)(2,1)S(1)} %constant_dynamic-update-slice_fusion), channel_id=1, source_target_pairs={{0,15},{1,0},{2,1},{3,2},{4,3},{5,4},{6,5},{7,6},{8,7},{9,8},{10,9... | collective-permute-start | bytes 368648 | tf_op jit(solution)/shard_map/ppermute | solution.py:17
  25.5 5.5 %collective-permute-start.2 = (bf16[96,640]{1,0:T(8,128)(2,1)S(1)}, bf16[96,640]{1,0:T(8,128)(2,1)S(1)}, u32[]{:S(2)}, u32[]{:S(2)}) collective-permute-start(bf16[96,640]{1,0:T(8,128)(2,1)S(1)} %collective-permute-done.1), channel_id=1, source_target_pairs={{0,1},{1,2},{2,3},{3,4},{4,5},{5,6},{6,7},{7,8},{8,9},{9,10},{10,1... | collective-permute-start | bytes 368648 | tf_op jit(solution)/shard_map/ppermute | solution.py:15
  25.5 5.5 %collective-permute-start.9 = (bf16[96,640]{1,0:T(8,128)(2,1)S(1)}, bf16[96,640]{1,0:T(8,128)(2,1)S(1)}, u32[]{:S(2)}, u32[]{:S(2)}) collective-permute-start(bf16[96,640]{1,0:T(8,128)(2,1)S(1)} %collective-permute-done.8), channel_id=1, source_target_pairs={{0,15},{1,0},{2,1},{3,2},{4,3},{5,4},{6,5},{7,6},{8,7},{9,8},{10,9... | collective-permute-start | bytes 368648 | tf_op jit(solution)/shard_map/ppermute | solution.py:17
  31.0 5.5 %collective-permute-start.3 = (bf16[96,640]{1,0:T(8,128)(2,1)S(1)}, bf16[96,640]{1,0:T(8,128)(2,1)S(1)}, u32[]{:S(2)}, u32[]{:S(2)}) collective-permute-start(bf16[96,640]{1,0:T(8,128)(2,1)S(1)} %collective-permute-done.2), channel_id=1, source_target_pairs={{0,1},{1,2},{2,3},{3,4},{4,5},{5,6},{6,7},{7,8},{8,9},{9,10},{10,1... | collective-permute-start | bytes 368648 | tf_op jit(solution)/shard_map/ppermute | solution.py:15
  31.0 5.5 %collective-permute-start.10 = (bf16[96,640]{1,0:T(8,128)(2,1)S(1)}, bf16[96,640]{1,0:T(8,128)(2,1)S(1)}, u32[]{:S(2)}, u32[]{:S(2)}) collective-permute-start(bf16[96,640]{1,0:T(8,128)(2,1)S(1)} %collective-permute-done.9), channel_id=1, source_target_pairs={{0,15},{1,0},{2,1},{3,2},{4,3},{5,4},{6,5},{7,6},{8,7},{9,8},{10,9... | collective-permute-start | bytes 368648 | tf_op jit(solution)/shard_map/ppermute | solution.py:17
  36.5 5.5 %collective-permute-start.4 = (bf16[96,640]{1,0:T(8,128)(2,1)S(1)}, bf16[96,640]{1,0:T(8,128)(2,1)S(1)}, u32[]{:S(2)}, u32[]{:S(2)}) collective-permute-start(bf16[96,640]{1,0:T(8,128)(2,1)S(1)} %collective-permute-done.3), channel_id=1, source_target_pairs={{0,1},{1,2},{2,3},{3,4},{4,5},{5,6},{6,7},{7,8},{8,9},{9,10},{10,1... | collective-permute-start | bytes 368648 | tf_op jit(solution)/shard_map/ppermute | solution.py:15
  36.5 5.5 %collective-permute-start.11 = (bf16[96,640]{1,0:T(8,128)(2,1)S(1)}, bf16[96,640]{1,0:T(8,128)(2,1)S(1)}, u32[]{:S(2)}, u32[]{:S(2)}) collective-permute-start(bf16[96,640]{1,0:T(8,128)(2,1)S(1)} %collective-permute-done.10), channel_id=1, source_target_pairs={{0,15},{1,0},{2,1},{3,2},{4,3},{5,4},{6,5},{7,6},{8,7},{9,8},{10,9... | collective-permute-start | bytes 368648 | tf_op jit(solution)/shard_map/ppermute | solution.py:17
  42.0 5.5 %collective-permute-start.5 = (bf16[96,640]{1,0:T(8,128)(2,1)S(1)}, bf16[96,640]{1,0:T(8,128)(2,1)S(1)}, u32[]{:S(2)}, u32[]{:S(2)}) collective-permute-start(bf16[96,640]{1,0:T(8,128)(2,1)S(1)} %collective-permute-done.4), channel_id=1, source_target_pairs={{0,1},{1,2},{2,3},{3,4},{4,5},{5,6},{6,7},{7,8},{8,9},{9,10},{10,1... | collective-permute-start | bytes 368648 | tf_op jit(solution)/shard_map/ppermute | solution.py:15
  42.0 7.1 %collective-permute-start.12 = (bf16[96,640]{1,0:T(8,128)(2,1)S(1)}, bf16[96,640]{1,0:T(8,128)(2,1)S(1)}, u32[]{:S(2)}, u32[]{:S(2)}) collective-permute-start(bf16[96,640]{1,0:T(8,128)(2,1)S(1)} %collective-permute-done.11), channel_id=1, source_target_pairs={{0,15},{1,0},{2,1},{3,2},{4,3},{5,4},{6,5},{7,6},{8,7},{9,8},{10,9... | collective-permute-start | bytes 368648 | tf_op jit(solution)/shard_map/ppermute | solution.py:17
  47.5 5.5 %collective-permute-start.6 = (bf16[96,640]{1,0:T(8,128)(2,1)S(1)}, bf16[96,640]{1,0:T(8,128)(2,1)S(1)}, u32[]{:S(2)}, u32[]{:S(2)}) collective-permute-start(bf16[96,640]{1,0:T(8,128)(2,1)S(1)} %collective-permute-done.5), channel_id=1, source_target_pairs={{0,1},{1,2},{2,3},{3,4},{4,5},{5,6},{6,7},{7,8},{8,9},{9,10},{10,1... | collective-permute-start | bytes 368648 | tf_op jit(solution)/shard_map/ppermute | solution.py:15
  49.2 5.4 %collective-permute-start.13 = (bf16[96,640]{1,0:T(8,128)(2,1)S(1)}, bf16[96,640]{1,0:T(8,128)(2,1)S(1)}, u32[]{:S(2)}, u32[]{:S(2)}) collective-permute-start(bf16[96,640]{1,0:T(8,128)(2,1)S(1)} %collective-permute-done.12), channel_id=1, source_target_pairs={{0,15},{1,0},{2,1},{3,2},{4,3},{5,4},{6,5},{7,6},{8,7},{9,8},{10,9... | collective-permute-start | bytes 368648 | tf_op jit(solution)/shard_map/ppermute | solution.py:17
  53.0 5.5 %collective-permute-start.7 = (bf16[96,640]{1,0:T(8,128)(2,1)S(1)}, bf16[96,640]{1,0:T(8,128)(2,1)S(1)}, u32[]{:S(2)}, u32[]{:S(2)}) collective-permute-start(bf16[96,640]{1,0:T(8,128)(2,1)S(1)} %collective-permute-done.6), channel_id=1, source_target_pairs={{0,1},{1,2},{2,3},{3,4},{4,5},{5,6},{6,7},{7,8},{8,9},{9,10},{10,1... | collective-permute-start | bytes 368648 | tf_op jit(solution)/shard_map/ppermute | solution.py:15
  54.3 8.6 %copy-start.9 = (bf16[96,512]{1,0:T(8,128)(2,1)S(1)}, bf16[96,512]{1,0:T(8,128)(2,1)}, u32[]{:S(2)}) copy-start(bf16[96,512]{1,0:T(8,128)(2,1)} %param.17) | copy-start | bytes 294916
  54.6 6.0 %collective-permute-start.14 = (bf16[96,640]{1,0:T(8,128)(2,1)S(1)}, bf16[96,640]{1,0:T(8,128)(2,1)S(1)}, u32[]{:S(2)}, u32[]{:S(2)}) collective-permute-start(bf16[96,640]{1,0:T(8,128)(2,1)S(1)} %collective-permute-done.13), channel_id=1, source_target_pairs={{0,15},{1,0},{2,1},{3,2},{4,3},{5,4},{6,5},{7,6},{8,7},{9,8},{10,9... | collective-permute-start | bytes 368648 | tf_op jit(solution)/shard_map/ppermute | solution.py:17
  60.4 3.2 %copy-start.5 = (bf16[96,1536]{1,0:T(8,128)(2,1)S(1)}, bf16[96,1536]{1,0:T(8,128)(2,1)}, u32[]{:S(2)}) copy-start(bf16[96,1536]{1,0:T(8,128)(2,1)} %param.11) | copy-start | bytes 884740
  60.7 5.0 %copy-start.2 = (bf16[2,256,256]{2,1,0:T(8,128)(2,1)S(1)}, bf16[2,256,256]{2,1,0:T(8,128)(2,1)}, u32[]{:S(2)}) copy-start(bf16[2,256,256]{2,1,0:T(8,128)(2,1)} %param.12) | copy-start | bytes 786436
  61.0 1.9 copy-start.1
  66.0 16.1 %copy-start.8 = (s32[64]{0:T(128)S(1)}, s32[64]{0:T(128)}, u32[]{:S(2)}) copy-start(s32[64]{0:T(128)} %param.16) | copy-start | bytes 772
  66.9 25.5 %copy-start.4 = (bf16[8,64,64]{2,1,0:T(8,128)(2,1)S(1)}, bf16[8,64,64]{2,1,0:T(8,128)(2,1)}, u32[]{:S(2)}) copy-start(bf16[8,64,64]{2,1,0:T(8,128)(2,1)} %param.13) | copy-start | bytes 196612
  69.7 24.0 %copy-start.7 = (bf16[96,128]{1,0:T(8,128)(2,1)S(1)}, bf16[96,128]{1,0:T(8,128)(2,1)}, u32[]{:S(2)}) copy-start(bf16[96,128]{1,0:T(8,128)(2,1)} %param.15) | copy-start | bytes 73732
  71.8 19.5 %all-to-all-start = ((bf16[32,2,2176]{2,1,0:T(2,128)(2,1)}), bf16[32,2,2176]{2,1,0:T(2,128)(2,1)S(1)}, u32[]{:S(2)}, u32[]{:S(2)}) async-start(bf16[32,2,2176]{2,1,0:T(2,128)(2,1)} %reshape.228), calls=%async_computation | async-start | bytes 557056 | tf_op jit(solution)/shard_map/all_to_all | solution.py:23
  95.6 16.1 %all-to-all-start.1 = ((bf16[32,2,2432]{2,1,0:T(2,128)(2,1)}), bf16[32,2,2432]{2,1,0:T(2,128)(2,1)S(1)}, u32[]{:S(2)}, u32[]{:S(2)}) async-start(bf16[32,2,2432]{2,1,0:T(2,128)(2,1)} %reshape.230), calls=%async_computation.1 | async-start | bytes 622592 | tf_op jit(solution)/shard_map/all_to_all | solution.py:23
  117.9 21.1 %all-to-all-start.2 = ((bf16[32,6,1536]{2,1,0:T(8,128)(2,1)}), bf16[32,6,1536]{2,1,0:T(8,128)(2,1)S(1)}, u32[]{:S(2)}, u32[]{:S(2)}) async-start(bf16[32,6,1536]{2,1,0:T(8,128)(2,1)} %convert_element_type.128), calls=%async_computation.2 | async-start | bytes 1572864 | tf_op jit(solution)/shard_map/all_to_all | solution.py:23
  124.2 64.9 %reduce-scatter.2.cloned.1.call-start = ((), (), s32[]{:S(2)}) async-start(), calls=%async_computation.5 | async-start | bytes 1253376 | tf_op jit(solution)/shard_map/reduce_scatter | solution.py:199
  140.5 53.0 %all-to-all-start.3 = ((f32[32,6,1536]{2,1,0:T(8,128)}), f32[32,6,1536]{2,1,0:T(8,128)S(1)}, u32[]{:S(2)}, u32[]{:S(2)}) async-start(f32[32,6,1536]{2,1,0:T(8,128)} %broadcast_in_dim.9), calls=%async_computation.3 | async-start | bytes 3145728 | tf_op jit(solution)/shard_map/all_to_all | solution.py:23
Sparse Core Ops, SparseCore 0:
  127.8 61.2 reduce-scatter.1
